TPU v7x, 256 devices: a whole 4x4x8 slice. The times are simulated.
256 devices in a mesh: seq: 64 (over z, x_lo, y), head: 4 (over x_hi, core).
Axes of the slice: x: 4 (x_hi: 2, x_lo: 2; x = x_hi * 2 + x_lo), y: 4, z: 8, core: 2. Of those that a mesh axis runs over, the one named last changes fastest.
Arguments:
- queries: bfloat16 [8192, 4096], P('seq', 'head')
- keys: bfloat16 [8192, 1024], P('seq', 'head')
- values: bfloat16 [8192, 1024], P('seq', 'head'), may hold values from -6 to 6
- out_weight: bfloat16 [4096, 4096], P('head'), may hold values from -0.09375 to 0.09375
- windows: int32 [32], replicated, may hold values from 512 to 2048, as said below
- seg_lengths: int32 [64], replicated, may hold values from 1 to 384, 8192 in all
- lang_ids: int32 [64], replicated, may hold values from 0 to 7
Outputs:
- centered: bfloat16 [8192, 4096], P('seq', 'head')
- pooled: float32 [64, 4096], P(None, 'head')
Inputs may be any that keep to these rules, and one draw needn't show every extreme that they name: `windows`: each head's window; some head has exactly 2048. `seg_lengths`: the spans tile the document; the longest is exactly 384.
All inputs are finite; a program needn't handle non-finite values.
Results may differ from a plain program's by a relative error of at most 0.014.
Values may be sent and summed in bfloat16 or wider, within the bound.
No kernel may reach another device: no remote copies, remote signals or barrier semaphores. Data moves between devices by JAX's collectives and lax.ppermute only.
A program may use at most 64 MiB of HBM per device.

v0:
```python
import jax
import jax.numpy as jnp
from jax import lax
from jax.sharding import PartitionSpec as P

HD = 128
NLANG = 8


def shifted(block, axis, distance):
    devices = range(lax.axis_size(axis))
    route = [(i - distance, i) for i in devices if i - distance in devices]
    return lax.ppermute(block, axis, route)


def on_device(queries, keys, values, out_weight, windows, seg_lengths, lang_ids):
    tok = queries.shape[0]
    q_heads = queries.shape[1] // HD
    kv_heads = keys.shape[1] // HD
    group = q_heads // kv_heads
    seq_count = lax.axis_size("seq")
    reach = min(16, seq_count // 2)
    total_len = tok * seq_count
    seq_me = lax.axis_index("seq")
    head_me = lax.axis_index("head")
    query_pos = seq_me * tok + jnp.arange(tok, dtype=jnp.int32)
    my_windows = lax.dynamic_slice_in_dim(windows, head_me * q_heads, q_heads).reshape(
        kv_heads, group
    )
    query_grid = queries.reshape(tok, kv_heads, group, HD)
    kv_cols = kv_heads * HD
    paired = jnp.concatenate([keys, values], axis=1)
    local_rows = jnp.arange(tok, dtype=jnp.int32)

    def absorb(state, block, key_pos):
        count = block.shape[0]
        key_block = block[:, :kv_cols].reshape(count, kv_heads, HD)
        value_block = block[:, kv_cols:].reshape(count, kv_heads, HD)
        scores = jnp.einsum(
            "tkgd,nkd->kgtn", query_grid, key_block, preferred_element_type=jnp.float32
        ) * HD ** (-0.5)
        distance = jnp.abs(query_pos[:, None] - key_pos[None, :])
        inside = (key_pos >= 0) & (key_pos < total_len)
        allowed = (distance[None, None] <= my_windows[:, :, None, None]) & inside[
            None, None, None, :
        ]
        scores = jnp.where(allowed, scores, jnp.float32(-1e30))
        top_old, total_old, accum = state
        top_new = jnp.maximum(top_old, jnp.max(scores, axis=-1))
        rescale = jnp.exp(top_old - top_new)
        probs = jnp.where(allowed, jnp.exp(scores - top_new[..., None]), jnp.float32(0.0))
        total_new = total_old * rescale + jnp.sum(probs, axis=-1)
        weighted = jnp.einsum(
            "kgtn,nkd->kgtd",
            probs.astype(jnp.bfloat16),
            value_block,
            preferred_element_type=jnp.float32,
        )
        return (top_new, total_new, accum * rescale[..., None] + weighted)

    state = (
        jnp.full((kv_heads, group, tok), -1e30, jnp.float32),
        jnp.zeros((kv_heads, group, tok), jnp.float32),
        jnp.zeros((kv_heads, group, tok, HD), jnp.float32),
    )
    state = absorb(state, paired, query_pos)
    factor = 4
    for first in range(1, reach + 1, factor):
        pieces = []
        places = []
        for step in range(first, first + factor):
            pieces.append(shifted(paired, "seq", step))
            places.append((seq_me - step) * tok + local_rows)
            pieces.append(shifted(paired, "seq", -step))
            places.append((seq_me + step) * tok + local_rows)
        state = absorb(state, jnp.concatenate(pieces, axis=0), jnp.concatenate(places, axis=0))
    top_final, total_final, accum = state
    mixed = accum / total_final[..., None]
    attn = mixed.transpose(2, 0, 1, 3).reshape(tok, q_heads * HD).astype(jnp.bfloat16)
    partial_sums = jnp.dot(attn, out_weight, preferred_element_type=jnp.float32)
    share_cols = out_weight.shape[1] // lax.axis_size("head")
    whole = lax.psum(partial_sums.astype(jnp.bfloat16), "head").astype(jnp.float32)
    tokens = lax.dynamic_slice_in_dim(whole, head_me * share_cols, share_cols, 1)
    ends = jnp.cumsum(seg_lengths)
    starts = ends - seg_lengths
    seg_hot = (
        (query_pos[:, None] >= starts[None, :]) & (query_pos[:, None] < ends[None, :])
    ).astype(jnp.float32)
    span_part = jnp.dot(seg_hot.T, tokens, precision=lax.Precision.HIGHEST)
    span_sum = lax.psum(span_part, "seq")
    lang_hot = (lang_ids[:, None] == jnp.arange(NLANG, dtype=jnp.int32)[None, :]).astype(
        jnp.float32
    )
    lang_sum = jnp.dot(lang_hot.T, span_sum, precision=lax.Precision.HIGHEST)
    lang_count = jnp.sum(lang_hot * seg_lengths.astype(jnp.float32)[:, None], axis=0)
    lang_mean = lang_sum / jnp.maximum(lang_count, 1.0)[:, None]
    seg_center = jnp.dot(lang_hot, lang_mean, precision=lax.Precision.HIGHEST)
    centered = (tokens - jnp.dot(seg_hot, seg_center, precision=lax.Precision.HIGHEST)).astype(
        jnp.bfloat16
    )
    pooled = span_sum / seg_lengths.astype(jnp.float32)[:, None] - seg_center
    return (centered, pooled)


def solution(mesh):
    in_specs = (
        P("seq", "head"),
        P("seq", "head"),
        P("seq", "head"),
        P("head", None),
        P(),
        P(),
        P(),
    )
    out_specs = (P("seq", "head"), P(None, "head"))
    return jax.shard_map(
        on_device, mesh=mesh, in_specs=in_specs, out_specs=out_specs, check_vma=False
    )
```

profile of v0, /device:TPU:4, one launch (start us, length us, event | category | flops | bytes accessed | tf_op | source)
XLA Modules:
  0.0 817.8 jit_solution(856714827481597212)
XLA Ops:
  9.1 4.8 collective-permute-start.16
  14.0 1.3 collective-permute-start.17
  15.3 7.1 collective-permute-start.18
  22.4 1.3 collective-permute-start.19
  23.7 6.8 collective-permute-start.20
  31.4 1.1 reshape.666
  34.8 1.3 collective-permute-start.21
  36.2 7.5 collective-permute-start.22
  43.8 1.3 collective-permute-start.23
  45.1 4.8 collective-permute-start.8
  50.0 1.3 collective-permute-start.9
  51.4 6.9 collective-permute-start.10
  58.3 1.3 collective-permute-start.11
  59.7 9.2 %collective-permute-start.12 = (bf16[128,512]{0,1:T(8,128)(2,1)S(1)}, bf16[128,512]{0,1:T(8,128)(2,1)S(1)}, u32[]{:S(2)}, u32[]{:S(2)}) collective-permute-start(bf16[128,512]{0,1:T(8,128)(2,1)S(1)} %pad_maximum_fusion), channel_id=1, source_target_pairs={{0,28},{4,32},{8,36},{12,40},{16,44},{20,48},{24,52},{28,56},{32,6... | collective-permute-start | bytes 393224 | tf_op jit(solution)/shard_map/ppermute | solution.py:13
  69.8 1.3 collective-permute-start.13
  71.2 9.3 %collective-permute-start.14 = (bf16[128,512]{0,1:T(8,128)(2,1)S(1)}, bf16[128,512]{0,1:T(8,128)(2,1)S(1)}, u32[]{:S(2)}, u32[]{:S(2)}) collective-permute-start(bf16[128,512]{0,1:T(8,128)(2,1)S(1)} %pad_maximum_fusion), channel_id=1, source_target_pairs={{0,32},{4,36},{8,40},{12,44},{16,48},{20,52},{24,56},{28,60},{32,6... | collective-permute-start | bytes 393224 | tf_op jit(solution)/shard_map/ppermute | solution.py:13
  80.5 1.3 collective-permute-start.15
  81.9 1.3 collective-permute-start
  83.2 1.3 collective-permute-start.1
  84.6 5.4 collective-permute-start.2
  90.0 1.3 collective-permute-start.3
  91.4 7.9 collective-permute-start.4
  100.2 1.3 collective-permute-start.5
  101.5 5.8 collective-permute-start.6
  107.4 1.3 collective-permute-start.7
  108.8 13.8 %collective-permute-start.24 = (bf16[128,512]{0,1:T(8,128)(2,1)S(1)}, bf16[128,512]{0,1:T(8,128)(2,1)S(1)}, u32[]{:S(2)}, u32[]{:S(2)}) collective-permute-start(bf16[128,512]{0,1:T(8,128)(2,1)S(1)} %pad_maximum_fusion), channel_id=1, source_target_pairs={{0,52},{4,56},{8,60},{12,64},{16,68},{20,72},{24,76},{28,80},{32,8... | collective-permute-start | bytes 393224 | tf_op jit(solution)/shard_map/ppermute | solution.py:13
  122.6 1.3 collective-permute-start.25
  124.0 11.2 %collective-permute-start.26 = (bf16[128,512]{0,1:T(8,128)(2,1)S(1)}, bf16[128,512]{0,1:T(8,128)(2,1)S(1)}, u32[]{:S(2)}, u32[]{:S(2)}) collective-permute-start(bf16[128,512]{0,1:T(8,128)(2,1)S(1)} %pad_maximum_fusion), channel_id=1, source_target_pairs={{0,56},{4,60},{8,64},{12,68},{16,72},{20,76},{24,80},{28,84},{32,8... | collective-permute-start | bytes 393224 | tf_op jit(solution)/shard_map/ppermute | solution.py:13
  135.2 1.3 collective-permute-start.27
  136.6 13.8 %collective-permute-start.28 = (bf16[128,512]{0,1:T(8,128)(2,1)S(1)}, bf16[128,512]{0,1:T(8,128)(2,1)S(1)}, u32[]{:S(2)}, u32[]{:S(2)}) collective-permute-start(bf16[128,512]{0,1:T(8,128)(2,1)S(1)} %pad_maximum_fusion), channel_id=1, source_target_pairs={{0,60},{4,64},{8,68},{12,72},{16,76},{20,80},{24,84},{28,88},{32,9... | collective-permute-start | bytes 393224 | tf_op jit(solution)/shard_map/ppermute | solution.py:13
  151.3 1.3 collective-permute-start.29
  152.7 3.7 collective-permute-start.30
  156.4 1.5 collective-permute-start.31
  158.1 3.1 collective-permute-done.29
  161.3 11.8 %collective-permute-done.31 = bf16[128,512]{0,1:T(8,128)(2,1)S(1)} collective-permute-done((bf16[128,512]{0,1:T(8,128)(2,1)S(1)}, bf16[128,512]{0,1:T(8,128)(2,1)S(1)}, u32[]{:S(2)}, u32[]{:S(2)}) %collective-permute-start.31) | collective-permute-done | bytes 131104 | tf_op jit(solution)/shard_map/ppermute | solution.py:13
  173.2 5.0 fusion.3
  178.2 1.6 fusion.29
  179.8 1.6 fusion.26
  181.6 7.3 fusion.56
  189.3 1.7 fusion.49
  191.0 1.6 fusion.52
  193.3 2.3 convolution_convert_fusion
  196.0 46.4 %all-reduce.3.cloned.1.call-done = bf16[128,4096]{1,0:T(8,128)(2,1)} async-done(((bf16[128,4096]{1,0:T(8,128)(2,1)}), bf16[128,4096]{1,0:T(8,128)(2,1)}) %all-reduce.3.cloned.1.call-update) | async-done | bytes 1048592 | tf_op jit(solution)/shard_map/psum | solution.py:82
  242.3 1.9 fusion.68
  244.4 561.4 %all-reduce.5.cloned.1.call-done = f32[64,1024]{1,0:T(8,128)} async-done(((f32[64,1024]{1,0:T(8,128)}), f32[64,1024]{1,0:T(8,128)}) %all-reduce.5.cloned.1.call-update) | async-done | bytes 262160 | tf_op jit(solution)/shard_map/psum | solution.py:90
  805.8 1.2 convolution_divide_fusion
  807.0 2.0 divide_subtract_fusion
  808.9 2.1 fusion.55
  (141 shorter events, 10.4 us)
Async XLA Ops:
  7.2 235.2 %all-reduce.3.cloned.1.call-start = ((), (), s32[]{:S(2)}) async-start(), calls=%async_computation | async-start | bytes 2097152 | tf_op jit(solution)/shard_map/psum | solution.py:82
  9.1 25.7 %collective-permute-start.16 = (bf16[128,512]{0,1:T(8,128)(2,1)S(1)}, bf16[128,512]{0,1:T(8,128)(2,1)S(1)}, u32[]{:S(2)}, u32[]{:S(2)}) collective-permute-start(bf16[128,512]{0,1:T(8,128)(2,1)S(1)} %pad_maximum_fusion), channel_id=1, source_target_pairs={{0,36},{4,40},{8,44},{12,48},{16,52},{20,56},{24,60},{28,64},{32,6... | collective-permute-start | bytes 393224 | tf_op jit(solution)/shard_map/ppermute | solution.py:13
  14.0 22.2 %collective-permute-start.17 = (bf16[128,512]{0,1:T(8,128)(2,1)S(1)}, bf16[128,512]{0,1:T(8,128)(2,1)S(1)}, u32[]{:S(2)}, u32[]{:S(2)}) collective-permute-start(bf16[128,512]{0,1:T(8,128)(2,1)S(1)} %pad_maximum_fusion), channel_id=1, source_target_pairs={{36,0},{40,4},{44,8},{48,12},{52,16},{56,20},{60,24},{64,28},{68,3... | collective-permute-start | bytes 393224 | tf_op jit(solution)/shard_map/ppermute | solution.py:13
  15.3 28.5 %collective-permute-start.18 = (bf16[128,512]{0,1:T(8,128)(2,1)S(1)}, bf16[128,512]{0,1:T(8,128)(2,1)S(1)}, u32[]{:S(2)}, u32[]{:S(2)}) collective-permute-start(bf16[128,512]{0,1:T(8,128)(2,1)S(1)} %pad_maximum_fusion), channel_id=1, source_target_pairs={{0,40},{4,44},{8,48},{12,52},{16,56},{20,60},{24,64},{28,68},{32,7... | collective-permute-start | bytes 393224 | tf_op jit(solution)/shard_map/ppermute | solution.py:13
  22.4 22.8 %collective-permute-start.19 = (bf16[128,512]{0,1:T(8,128)(2,1)S(1)}, bf16[128,512]{0,1:T(8,128)(2,1)S(1)}, u32[]{:S(2)}, u32[]{:S(2)}) collective-permute-start(bf16[128,512]{0,1:T(8,128)(2,1)S(1)} %pad_maximum_fusion), channel_id=1, source_target_pairs={{40,0},{44,4},{48,8},{52,12},{56,16},{60,20},{64,24},{68,28},{72,3... | collective-permute-start | bytes 393224 | tf_op jit(solution)/shard_map/ppermute | solution.py:13
  23.7 26.3 %collective-permute-start.20 = (bf16[128,512]{0,1:T(8,128)(2,1)S(1)}, bf16[128,512]{0,1:T(8,128)(2,1)S(1)}, u32[]{:S(2)}, u32[]{:S(2)}) collective-permute-start(bf16[128,512]{0,1:T(8,128)(2,1)S(1)} %pad_maximum_fusion), channel_id=1, source_target_pairs={{0,44},{4,48},{8,52},{12,56},{16,60},{20,64},{24,68},{28,72},{32,7... | collective-permute-start | bytes 393224 | tf_op jit(solution)/shard_map/ppermute | solution.py:13
  34.8 16.5 %collective-permute-start.21 = (bf16[128,512]{0,1:T(8,128)(2,1)S(1)}, bf16[128,512]{0,1:T(8,128)(2,1)S(1)}, u32[]{:S(2)}, u32[]{:S(2)}) collective-permute-start(bf16[128,512]{0,1:T(8,128)(2,1)S(1)} %pad_maximum_fusion), channel_id=1, source_target_pairs={{44,0},{48,4},{52,8},{56,12},{60,16},{64,20},{68,24},{72,28},{76,3... | collective-permute-start | bytes 393224 | tf_op jit(solution)/shard_map/ppermute | solution.py:13
  36.2 22.1 %collective-permute-start.22 = (bf16[128,512]{0,1:T(8,128)(2,1)S(1)}, bf16[128,512]{0,1:T(8,128)(2,1)S(1)}, u32[]{:S(2)}, u32[]{:S(2)}) collective-permute-start(bf16[128,512]{0,1:T(8,128)(2,1)S(1)} %pad_maximum_fusion), channel_id=1, source_target_pairs={{0,48},{4,52},{8,56},{12,60},{16,64},{20,68},{24,72},{28,76},{32,8... | collective-permute-start | bytes 393224 | tf_op jit(solution)/shard_map/ppermute | solution.py:13
  43.8 15.9 %collective-permute-start.23 = (bf16[128,512]{0,1:T(8,128)(2,1)S(1)}, bf16[128,512]{0,1:T(8,128)(2,1)S(1)}, u32[]{:S(2)}, u32[]{:S(2)}) collective-permute-start(bf16[128,512]{0,1:T(8,128)(2,1)S(1)} %pad_maximum_fusion), channel_id=1, source_target_pairs={{48,0},{52,4},{56,8},{60,12},{64,16},{68,20},{72,24},{76,28},{80,3... | collective-permute-start | bytes 393224 | tf_op jit(solution)/shard_map/ppermute | solution.py:13
  45.1 24.7 %collective-permute-start.8 = (bf16[128,512]{0,1:T(8,128)(2,1)S(1)}, bf16[128,512]{0,1:T(8,128)(2,1)S(1)}, u32[]{:S(2)}, u32[]{:S(2)}) collective-permute-start(bf16[128,512]{0,1:T(8,128)(2,1)S(1)} %pad_maximum_fusion), channel_id=1, source_target_pairs={{0,20},{4,24},{8,28},{12,32},{16,36},{20,40},{24,44},{28,48},{32,5... | collective-permute-start | bytes 393224 | tf_op jit(solution)/shard_map/ppermute | solution.py:13
  50.0 21.1 %collective-permute-start.9 = (bf16[128,512]{0,1:T(8,128)(2,1)S(1)}, bf16[128,512]{0,1:T(8,128)(2,1)S(1)}, u32[]{:S(2)}, u32[]{:S(2)}) collective-permute-start(bf16[128,512]{0,1:T(8,128)(2,1)S(1)} %pad_maximum_fusion), channel_id=1, source_target_pairs={{20,0},{24,4},{28,8},{32,12},{36,16},{40,20},{44,24},{48,28},{52,3... | collective-permute-start | bytes 393224 | tf_op jit(solution)/shard_map/ppermute | solution.py:13
  51.4 29.1 %collective-permute-start.10 = (bf16[128,512]{0,1:T(8,128)(2,1)S(1)}, bf16[128,512]{0,1:T(8,128)(2,1)S(1)}, u32[]{:S(2)}, u32[]{:S(2)}) collective-permute-start(bf16[128,512]{0,1:T(8,128)(2,1)S(1)} %pad_maximum_fusion), channel_id=1, source_target_pairs={{0,24},{4,28},{8,32},{12,36},{16,40},{20,44},{24,48},{28,52},{32,5... | collective-permute-start | bytes 393224 | tf_op jit(solution)/shard_map/ppermute | solution.py:13
  58.3 23.5 %collective-permute-start.11 = (bf16[128,512]{0,1:T(8,128)(2,1)S(1)}, bf16[128,512]{0,1:T(8,128)(2,1)S(1)}, u32[]{:S(2)}, u32[]{:S(2)}) collective-permute-start(bf16[128,512]{0,1:T(8,128)(2,1)S(1)} %pad_maximum_fusion), channel_id=1, source_target_pairs={{24,0},{28,4},{32,8},{36,12},{40,16},{44,20},{48,24},{52,28},{56,3... | collective-permute-start | bytes 393224 | tf_op jit(solution)/shard_map/ppermute | solution.py:13
  59.7 23.5 %collective-permute-start.12 = (bf16[128,512]{0,1:T(8,128)(2,1)S(1)}, bf16[128,512]{0,1:T(8,128)(2,1)S(1)}, u32[]{:S(2)}, u32[]{:S(2)}) collective-permute-start(bf16[128,512]{0,1:T(8,128)(2,1)S(1)} %pad_maximum_fusion), channel_id=1, source_target_pairs={{0,28},{4,32},{8,36},{12,40},{16,44},{20,48},{24,52},{28,56},{32,6... | collective-permute-start | bytes 393224 | tf_op jit(solution)/shard_map/ppermute | solution.py:13
  69.8 14.8 %collective-permute-start.13 = (bf16[128,512]{0,1:T(8,128)(2,1)S(1)}, bf16[128,512]{0,1:T(8,128)(2,1)S(1)}, u32[]{:S(2)}, u32[]{:S(2)}) collective-permute-start(bf16[128,512]{0,1:T(8,128)(2,1)S(1)} %pad_maximum_fusion), channel_id=1, source_target_pairs={{28,0},{32,4},{36,8},{40,12},{44,16},{48,20},{52,24},{56,28},{60,3... | collective-permute-start | bytes 393224 | tf_op jit(solution)/shard_map/ppermute | solution.py:13
  71.2 18.8 %collective-permute-start.14 = (bf16[128,512]{0,1:T(8,128)(2,1)S(1)}, bf16[128,512]{0,1:T(8,128)(2,1)S(1)}, u32[]{:S(2)}, u32[]{:S(2)}) collective-permute-start(bf16[128,512]{0,1:T(8,128)(2,1)S(1)} %pad_maximum_fusion), channel_id=1, source_target_pairs={{0,32},{4,36},{8,40},{12,44},{16,48},{20,52},{24,56},{28,60},{32,6... | collective-permute-start | bytes 393224 | tf_op jit(solution)/shard_map/ppermute | solution.py:13
  80.5 10.8 %collective-permute-start.15 = (bf16[128,512]{0,1:T(8,128)(2,1)S(1)}, bf16[128,512]{0,1:T(8,128)(2,1)S(1)}, u32[]{:S(2)}, u32[]{:S(2)}) collective-permute-start(bf16[128,512]{0,1:T(8,128)(2,1)S(1)} %pad_maximum_fusion), channel_id=1, source_target_pairs={{32,0},{36,4},{40,8},{44,12},{48,16},{52,20},{56,24},{60,28},{64,3... | collective-permute-start | bytes 393224 | tf_op jit(solution)/shard_map/ppermute | solution.py:13
  81.9 18.3 %collective-permute-start = (bf16[128,512]{0,1:T(8,128)(2,1)S(1)}, bf16[128,512]{0,1:T(8,128)(2,1)S(1)}, u32[]{:S(2)}, u32[]{:S(2)}) collective-permute-start(bf16[128,512]{0,1:T(8,128)(2,1)S(1)} %pad_maximum_fusion), channel_id=1, source_target_pairs={{0,4},{4,8},{8,12},{12,16},{16,20},{20,24},{24,28},{28,32},{32,36}... | collective-permute-start | bytes 393224 | tf_op jit(solution)/shard_map/ppermute | solution.py:13
  83.2 18.3 %collective-permute-start.1 = (bf16[128,512]{0,1:T(8,128)(2,1)S(1)}, bf16[128,512]{0,1:T(8,128)(2,1)S(1)}, u32[]{:S(2)}, u32[]{:S(2)}) collective-permute-start(bf16[128,512]{0,1:T(8,128)(2,1)S(1)} %pad_maximum_fusion), channel_id=1, source_target_pairs={{4,0},{8,4},{12,8},{16,12},{20,16},{24,20},{28,24},{32,28},{36,32}... | collective-permute-start | bytes 393224 | tf_op jit(solution)/shard_map/ppermute | solution.py:13
  84.6 22.8 %collective-permute-start.2 = (bf16[128,512]{0,1:T(8,128)(2,1)S(1)}, bf16[128,512]{0,1:T(8,128)(2,1)S(1)}, u32[]{:S(2)}, u32[]{:S(2)}) collective-permute-start(bf16[128,512]{0,1:T(8,128)(2,1)S(1)} %pad_maximum_fusion), channel_id=1, source_target_pairs={{0,8},{4,12},{8,16},{12,20},{16,24},{20,28},{24,32},{28,36},{32,40... | collective-permute-start | bytes 393224 | tf_op jit(solution)/shard_map/ppermute | solution.py:13
  90.0 18.7 %collective-permute-start.3 = (bf16[128,512]{0,1:T(8,128)(2,1)S(1)}, bf16[128,512]{0,1:T(8,128)(2,1)S(1)}, u32[]{:S(2)}, u32[]{:S(2)}) collective-permute-start(bf16[128,512]{0,1:T(8,128)(2,1)S(1)} %pad_maximum_fusion), channel_id=1, source_target_pairs={{8,0},{12,4},{16,8},{20,12},{24,16},{28,20},{32,24},{36,28},{40,32... | collective-permute-start | bytes 393224 | tf_op jit(solution)/shard_map/ppermute | solution.py:13
  91.4 31.3 %collective-permute-start.4 = (bf16[128,512]{0,1:T(8,128)(2,1)S(1)}, bf16[128,512]{0,1:T(8,128)(2,1)S(1)}, u32[]{:S(2)}, u32[]{:S(2)}) collective-permute-start(bf16[128,512]{0,1:T(8,128)(2,1)S(1)} %pad_maximum_fusion), channel_id=1, source_target_pairs={{0,12},{4,16},{8,20},{12,24},{16,28},{20,32},{24,36},{28,40},{32,4... | collective-permute-start | bytes 393224 | tf_op jit(solution)/shard_map/ppermute | solution.py:13
  100.2 23.8 %collective-permute-start.5 = (bf16[128,512]{0,1:T(8,128)(2,1)S(1)}, bf16[128,512]{0,1:T(8,128)(2,1)S(1)}, u32[]{:S(2)}, u32[]{:S(2)}) collective-permute-start(bf16[128,512]{0,1:T(8,128)(2,1)S(1)} %pad_maximum_fusion), channel_id=1, source_target_pairs={{12,0},{16,4},{20,8},{24,12},{28,16},{32,20},{36,24},{40,28},{44,3... | collective-permute-start | bytes 393224 | tf_op jit(solution)/shard_map/ppermute | solution.py:13
  101.5 33.7 %collective-permute-start.6 = (bf16[128,512]{0,1:T(8,128)(2,1)S(1)}, bf16[128,512]{0,1:T(8,128)(2,1)S(1)}, u32[]{:S(2)}, u32[]{:S(2)}) collective-permute-start(bf16[128,512]{0,1:T(8,128)(2,1)S(1)} %pad_maximum_fusion), channel_id=1, source_target_pairs={{0,16},{4,20},{8,24},{12,28},{16,32},{20,36},{24,40},{28,44},{32,4... | collective-permute-start | bytes 393224 | tf_op jit(solution)/shard_map/ppermute | solution.py:13
  107.4 29.2 %collective-permute-start.7 = (bf16[128,512]{0,1:T(8,128)(2,1)S(1)}, bf16[128,512]{0,1:T(8,128)(2,1)S(1)}, u32[]{:S(2)}, u32[]{:S(2)}) collective-permute-start(bf16[128,512]{0,1:T(8,128)(2,1)S(1)} %pad_maximum_fusion), channel_id=1, source_target_pairs={{16,0},{20,4},{24,8},{28,12},{32,16},{36,20},{40,24},{44,28},{48,3... | collective-permute-start | bytes 393224 | tf_op jit(solution)/shard_map/ppermute | solution.py:13
  108.8 42.6 %collective-permute-start.24 = (bf16[128,512]{0,1:T(8,128)(2,1)S(1)}, bf16[128,512]{0,1:T(8,128)(2,1)S(1)}, u32[]{:S(2)}, u32[]{:S(2)}) collective-permute-start(bf16[128,512]{0,1:T(8,128)(2,1)S(1)} %pad_maximum_fusion), channel_id=1, source_target_pairs={{0,52},{4,56},{8,60},{12,64},{16,68},{20,72},{24,76},{28,80},{32,8... | collective-permute-start | bytes 393224 | tf_op jit(solution)/shard_map/ppermute | solution.py:13
  122.6 30.0 %collective-permute-start.25 = (bf16[128,512]{0,1:T(8,128)(2,1)S(1)}, bf16[128,512]{0,1:T(8,128)(2,1)S(1)}, u32[]{:S(2)}, u32[]{:S(2)}) collective-permute-start(bf16[128,512]{0,1:T(8,128)(2,1)S(1)} %pad_maximum_fusion), channel_id=1, source_target_pairs={{52,0},{56,4},{60,8},{64,12},{68,16},{72,20},{76,24},{80,28},{84,3... | collective-permute-start | bytes 393224 | tf_op jit(solution)/shard_map/ppermute | solution.py:13
  124.0 32.4 %collective-permute-start.26 = (bf16[128,512]{0,1:T(8,128)(2,1)S(1)}, bf16[128,512]{0,1:T(8,128)(2,1)S(1)}, u32[]{:S(2)}, u32[]{:S(2)}) collective-permute-start(bf16[128,512]{0,1:T(8,128)(2,1)S(1)} %pad_maximum_fusion), channel_id=1, source_target_pairs={{0,56},{4,60},{8,64},{12,68},{16,72},{20,76},{24,80},{28,84},{32,8... | collective-permute-start | bytes 393224 | tf_op jit(solution)/shard_map/ppermute | solution.py:13
  135.2 22.7 %collective-permute-start.27 = (bf16[128,512]{0,1:T(8,128)(2,1)S(1)}, bf16[128,512]{0,1:T(8,128)(2,1)S(1)}, u32[]{:S(2)}, u32[]{:S(2)}) collective-permute-start(bf16[128,512]{0,1:T(8,128)(2,1)S(1)} %pad_maximum_fusion), channel_id=1, source_target_pairs={{56,0},{60,4},{64,8},{68,12},{72,16},{76,20},{80,24},{84,28},{88,3... | collective-permute-start | bytes 393224 | tf_op jit(solution)/shard_map/ppermute | solution.py:13
  136.6 21.4 %collective-permute-start.28 = (bf16[128,512]{0,1:T(8,128)(2,1)S(1)}, bf16[128,512]{0,1:T(8,128)(2,1)S(1)}, u32[]{:S(2)}, u32[]{:S(2)}) collective-permute-start(bf16[128,512]{0,1:T(8,128)(2,1)S(1)} %pad_maximum_fusion), channel_id=1, source_target_pairs={{0,60},{4,64},{8,68},{12,72},{16,76},{20,80},{24,84},{28,88},{32,9... | collective-permute-start | bytes 393224 | tf_op jit(solution)/shard_map/ppermute | solution.py:13
  151.3 9.9 %collective-permute-start.29 = (bf16[128,512]{0,1:T(8,128)(2,1)S(1)}, bf16[128,512]{0,1:T(8,128)(2,1)S(1)}, u32[]{:S(2)}, u32[]{:S(2)}) collective-permute-start(bf16[128,512]{0,1:T(8,128)(2,1)S(1)} %pad_maximum_fusion), channel_id=1, source_target_pairs={{60,0},{64,4},{68,8},{72,12},{76,16},{80,20},{84,24},{88,28},{92,3... | collective-permute-start | bytes 393224 | tf_op jit(solution)/shard_map/ppermute | solution.py:13
  152.7 8.6 %collective-permute-start.30 = (bf16[128,512]{0,1:T(8,128)(2,1)S(1)}, bf16[128,512]{0,1:T(8,128)(2,1)S(1)}, u32[]{:S(2)}, u32[]{:S(2)}) collective-permute-start(bf16[128,512]{0,1:T(8,128)(2,1)S(1)} %pad_maximum_fusion), channel_id=1, source_target_pairs={{0,64},{4,68},{8,72},{12,76},{16,80},{20,84},{24,88},{28,92},{32,9... | collective-permute-start | bytes 393224 | tf_op jit(solution)/shard_map/ppermute | solution.py:13
  156.4 16.7 %collective-permute-start.31 = (bf16[128,512]{0,1:T(8,128)(2,1)S(1)}, bf16[128,512]{0,1:T(8,128)(2,1)S(1)}, u32[]{:S(2)}, u32[]{:S(2)}) collective-permute-start(bf16[128,512]{0,1:T(8,128)(2,1)S(1)} %pad_maximum_fusion), channel_id=1, source_target_pairs={{64,0},{68,4},{72,8},{76,12},{80,16},{84,20},{88,24},{92,28},{96,3... | collective-permute-start | bytes 393224 | tf_op jit(solution)/shard_map/ppermute | solution.py:13
  189.3 3.3 slice-start
  191.0 2.3 slice-start.1
  193.3 2.4 copy-start
  193.3 51.0 %copy-start.1 = (s32[64]{0:T(128)S(1)}, s32[64]{0:T(128)}, u32[]{:S(2)}) copy-start(s32[64]{0:T(128)} %param.13) | copy-start | bytes 772
  195.6 610.2 %all-reduce.5.cloned.1.call-start = ((), (), s32[]{:S(2)}) async-start(), calls=%async_computation.1 | async-start | bytes 524288 | tf_op jit(solution)/shard_map/psum | solution.py:90
Sparse Core Ops, SparseCore 0:
  195.7 46.5 all-reduce.2
  245.5 560.2 all-reduce.4
where the time goes:
time: 819 us; the launch traced here: 818 us
  waiting for transfers between devices  623 us (76%)
  starting transfers between devices  140 us (17%)
  matrix products  23.7 us (3%)
  between operations  15.3 us (2%)
  other arithmetic  8.83 us (1%)
    psum x1, waiting for transfers between devices, on_device(): span_sum = lax.psum(span_part, 'seq')  561 us
    ppermute x32, starting transfers between devices, shifted(): return lax.ppermute(block, axis, route)  140 us
    psum x1, waiting for transfers between devices, on_device(): lax.psum(partial_sums.astype(jnp.bfloat16), 'head').astype(jnp.float32)  46.4 us
  transfers between devices with their start and end apart: 34, of which 4 were waited for; matrix products, arithmetic and copies ran while one was open for 1% of the time, Pallas kernels for 0%

commit v1 on v0

v1 whole, which is shorter than its diff:
```python
import math

import jax
import jax.numpy as jnp
from jax import lax
from jax.experimental import pallas as pl
from jax.experimental.pallas import tpu as pltpu
from jax.sharding import Mesh, PartitionSpec as P

HD = 128
NLANG = 8
NZ, NXL, NY, NXH, NCORE = 8, 2, 4, 2, 2
PLANE = NXL * NY
TOK = 128
T = PLANE * TOK
REACH = 2048
NK = T + 2 * REACH
SEGS = 64
SPZ = SEGS // NZ
ROWS = TOK + 2 * SPZ
COLS = 1024
NEG = -1e30
EXPC = HD**-0.5 / math.log(2.0)
BQ = 512
BK = 1024


def seg_bounds(lens):
    row = lax.broadcasted_iota(jnp.int32, (SEGS, SEGS), 0)
    col = lax.broadcasted_iota(jnp.int32, (SEGS, SEGS), 1)
    ends = jnp.sum(jnp.where(col <= row, lens, 0.0), axis=1, keepdims=True)
    starts = jnp.sum(jnp.where(col < row, lens, 0.0), axis=1, keepdims=True)
    return starts, ends


def attn_kernel(sc_ref, own_ref, dn_ref, up_ref, a2_ref, len_ref, o_ref, s_ref, kbuf, vbuf, sbuf):
    w = sc_ref[0]
    z = sc_ref[1]
    kbuf[0:T, :] = a2_ref[:, HD : 2 * HD]
    vbuf[0:T, :] = a2_ref[:, 2 * HD : 3 * HD]
    kbuf[T : 2 * T, :] = dn_ref[:, 0:HD]
    vbuf[T : 2 * T, :] = dn_ref[:, HD : 2 * HD]
    kbuf[2 * T : 3 * T, :] = own_ref[:, 0:HD]
    vbuf[2 * T : 3 * T, :] = own_ref[:, HD : 2 * HD]
    kbuf[3 * T : 4 * T, :] = up_ref[:, 0:HD]
    vbuf[3 * T : 4 * T, :] = up_ref[:, HD : 2 * HD]
    kbuf[4 * T : 5 * T, :] = a2_ref[:, 3 * HD : 4 * HD]
    vbuf[4 * T : 5 * T, :] = a2_ref[:, 4 * HD : 5 * HD]
    lo_valid = jnp.maximum(0, REACH - z * T)
    hi_valid = jnp.minimum(NK, REACH + (NZ - z) * T)
    diff = lax.broadcasted_iota(jnp.int32, (BQ, BK), 0) - lax.broadcasted_iota(
        jnp.int32, (BQ, BK), 1
    )

    def qloop(qb, _):
        qs = pl.multiple_of(qb * BQ, BQ)
        q = a2_ref[pl.ds(qs, BQ), 0:HD]
        qf = qs + REACH
        ql = qf + BQ - 1
        lo = jnp.maximum(qf - w, lo_valid)
        hi = jnp.minimum(ql + w + 1, hi_valid)
        b_lo = lo // BK
        b_hi = (hi + BK - 1) // BK
        b_il = jnp.clip((jnp.maximum(ql - w, 0) + BK - 1) // BK, b_lo, b_hi)
        b_ih = jnp.clip((qf + w + 1) // BK, b_il, b_hi)

        def qk(b, mx, masked):
            k0 = pl.multiple_of(b * BK, BK)
            s = lax.dot_general(
                q,
                kbuf[pl.ds(k0, BK), :],
                (((1,), (1,)), ((), ())),
                preferred_element_type=jnp.float32,
            )
            if masked:
                s = jnp.where(jnp.abs(diff + (qf - k0)) <= w, s, NEG)
            sbuf[b] = s
            for c in range(BK // 128):
                mx = jnp.maximum(mx, s[:, c * 128 : (c + 1) * 128])
            return mx

        mx = jnp.full((BQ, 128), NEG, jnp.float32)
        mx = lax.fori_loop(b_lo, b_il, lambda b, c: qk(b, c, True), mx)
        mx = lax.fori_loop(b_il, b_ih, lambda b, c: qk(b, c, False), mx)
        mx = lax.fori_loop(b_ih, b_hi, lambda b, c: qk(b, c, True), mx)
        m = jnp.max(mx, axis=1, keepdims=True)

        def pv(b, carry):
            total, acc = carry
            k0 = pl.multiple_of(b * BK, BK)
            p = jnp.exp2((sbuf[b] - m) * EXPC)
            for c in range(BK // 128):
                total = total + p[:, c * 128 : (c + 1) * 128]
            acc = acc + lax.dot_general(
                p.astype(jnp.bfloat16),
                vbuf[pl.ds(k0, BK), :],
                (((1,), (0,)), ((), ())),
                preferred_element_type=jnp.float32,
            )
            return total, acc

        total, acc = lax.fori_loop(
            b_lo,
            b_hi,
            pv,
            (jnp.zeros((BQ, 128), jnp.float32), jnp.zeros((BQ, HD), jnp.float32)),
        )
        denom = jnp.sum(total, axis=1, keepdims=True)
        o_ref[pl.ds(qs, BQ), :] = (acc / denom).astype(jnp.bfloat16)
        return 0

    lax.fori_loop(0, T // BQ, qloop, 0)
    starts, ends = seg_bounds(len_ref[...].astype(jnp.float32))
    pos = (lax.broadcasted_iota(jnp.int32, (SEGS, T), 1) + z * T).astype(jnp.float32)
    hot = jnp.where((pos >= starts) & (pos < ends), 1.0, 0.0).astype(jnp.bfloat16)
    s_ref[...] = jnp.dot(hot, o_ref[...], preferred_element_type=jnp.float32)


def attention(scalars, own, down, up, mixed, lens_row):
    vmem = pl.BlockSpec(memory_space=pltpu.VMEM)
    return pl.pallas_call(
        attn_kernel,
        out_shape=(
            jax.ShapeDtypeStruct((T, HD), jnp.bfloat16),
            jax.ShapeDtypeStruct((SEGS, HD), jnp.float32),
        ),
        in_specs=[pl.BlockSpec(memory_space=pltpu.SMEM), vmem, vmem, vmem, vmem, vmem],
        out_specs=(vmem, vmem),
        scratch_shapes=[
            pltpu.VMEM((NK, HD), jnp.bfloat16),
            pltpu.VMEM((NK, HD), jnp.bfloat16),
            pltpu.VMEM((NK // BK, BQ, BK), jnp.float32),
        ],
        name="window_attention",
    )(scalars, own, down, up, mixed, lens_row)


def proj_kernel(x_ref, w_ref, o_ref):
    acc = jnp.zeros((ROWS, COLS), jnp.float32)
    for r in range(PLANE):
        acc = acc + jnp.dot(
            x_ref[r], w_ref[r * HD : (r + 1) * HD, :], preferred_element_type=jnp.float32
        )
    hi, lo = split_rows(acc[TOK : TOK + SPZ] + acc[TOK + SPZ :])
    o_ref[0, 0, 0:TOK, :] = acc[0:TOK].astype(jnp.bfloat16)
    o_ref[0, 0, TOK:ROWS, :] = jnp.concatenate([hi, lo], axis=0).astype(jnp.bfloat16)


def split_rows(x):
    hi = x.astype(jnp.bfloat16).astype(jnp.float32)
    return hi, x - hi


def project(x, out_weight):
    return pl.pallas_call(
        proj_kernel,
        grid=(NXH * NCORE,),
        out_shape=jax.ShapeDtypeStruct((NCORE, NXH, ROWS, COLS), jnp.bfloat16),
        in_specs=[
            pl.BlockSpec((PLANE, ROWS, HD), lambda j: (0, 0, 0)),
            pl.BlockSpec((PLANE * HD, COLS), lambda j: (0, j)),
        ],
        out_specs=pl.BlockSpec((1, 1, ROWS, COLS), lambda j: (j % NCORE, j // NCORE, 0, 0)),
        name="projection",
    )(x, out_weight)


def merge_kernel(y_ref, o_ref):
    acc = y_ref[0, 0].astype(jnp.float32) + y_ref[1, 0].astype(jnp.float32)
    hi, lo = split_rows(acc[TOK : TOK + SPZ] + acc[TOK + SPZ :])
    o_ref[0, 0:TOK, :] = acc[0:TOK].astype(jnp.bfloat16)
    o_ref[0, TOK:ROWS, :] = jnp.concatenate([hi, lo], axis=0).astype(jnp.bfloat16)


def merge(y):
    return pl.pallas_call(
        merge_kernel,
        grid=(NXH,),
        out_shape=jax.ShapeDtypeStruct((NXH, ROWS, COLS), jnp.bfloat16),
        in_specs=[pl.BlockSpec((NCORE, 1, ROWS, COLS), lambda j: (0, j, 0, 0))],
        out_specs=pl.BlockSpec((1, ROWS, COLS), lambda j: (j, 0, 0)),
        name="merge",
    )(y)


def final_kernel(sc_ref, y_ref, span_ref, len_ref, lenc_ref, idr_ref, idc_ref, c_ref, p_ref):
    base = sc_ref[2]
    lens = len_ref[...].astype(jnp.float32)
    starts, ends = seg_bounds(lens)
    pos = (lax.broadcasted_iota(jnp.int32, (SEGS, TOK), 1) + base).astype(jnp.float32)
    hot = jnp.where((pos >= starts) & (pos < ends), 1.0, 0.0)
    same = jnp.where(idc_ref[...] == idr_ref[...], 1.0, 0.0)
    count = jnp.maximum(jnp.sum(same * lens, axis=1, keepdims=True), 1.0)
    spans = span_ref[...]
    center = (
        jnp.dot(
            same, spans, precision=lax.Precision.HIGHEST, preferred_element_type=jnp.float32
        )
        / count
    )
    p_ref[...] = spans / lenc_ref[...].astype(jnp.float32) - center
    tokens = y_ref[0, 0:TOK, :].astype(jnp.float32) + y_ref[1, 0:TOK, :].astype(jnp.float32)
    mean = lax.dot_general(
        hot,
        center,
        (((0,), (0,)), ((), ())),
        precision=lax.Precision.HIGHEST,
        preferred_element_type=jnp.float32,
    )
    c_ref[...] = (tokens - mean).astype(jnp.bfloat16)


def finalize(scalars, y, spans, seg_lengths, lang_ids):
    vmem = pl.BlockSpec(memory_space=pltpu.VMEM)
    return pl.pallas_call(
        final_kernel,
        out_shape=(
            jax.ShapeDtypeStruct((TOK, COLS), jnp.bfloat16),
            jax.ShapeDtypeStruct((SEGS, COLS), jnp.float32),
        ),
        in_specs=[pl.BlockSpec(memory_space=pltpu.SMEM)] + [vmem] * 6,
        out_specs=(vmem, vmem),
        name="centre",
    )(
        scalars,
        y,
        spans,
        seg_lengths.reshape(1, SEGS),
        seg_lengths.reshape(SEGS, 1),
        lang_ids.reshape(1, SEGS),
        lang_ids.reshape(SEGS, 1),
    )


def shifted(block, axis, distance):
    devices = range(lax.axis_size(axis))
    route = [(i - distance, i) for i in devices if i - distance in devices]
    return lax.ppermute(block, axis, route)


def exchange(x, axes):
    return lax.all_to_all(x, axes, 0, 0, tiled=True)


def on_device(queries, keys, values, out_weight, windows, seg_lengths, lang_ids):
    plane_axes = ("xl", "y")
    z = lax.axis_index("z")
    rank = lax.axis_index("xl") * NY + lax.axis_index("y")
    head = (lax.axis_index("xh") * NCORE + lax.axis_index("core")) * PLANE + rank
    window = lax.dynamic_index_in_dim(windows, head, keepdims=False)
    scalars = jnp.stack([window, z, (z * PLANE + rank) * TOK]).astype(jnp.int32)
    raw = jnp.stack(
        [
            jnp.concatenate([keys[:, j * HD : (j + 1) * HD], values[:, j * HD : (j + 1) * HD]], 1)
            for j in range(2)
        ]
    )
    far_down = shifted(raw, "z", 2)
    far_up = shifted(raw, "z", -2)
    own = exchange(jnp.repeat(raw, PLANE // 2, axis=0), plane_axes).reshape(T, 2 * HD)
    down = shifted(own, "z", 1)
    up = shifted(own, "z", -1)
    by_head = queries.reshape(TOK, PLANE, HD).transpose(1, 0, 2)
    mixed = jnp.concatenate(
        [by_head, jnp.repeat(far_down, PLANE // 2, axis=0), jnp.repeat(far_up, PLANE // 2, axis=0)],
        axis=2,
    )
    mixed = exchange(mixed, plane_axes).reshape(T, 5 * HD)
    attn, span_attn = attention(scalars, own, down, up, mixed, seg_lengths.reshape(1, SEGS))
    span_mine = jnp.sum(exchange(span_attn.reshape(NZ, SPZ, HD), "z"), axis=0)
    hi, lo = split_rows(span_mine)
    span_rows = jnp.concatenate([hi, lo], axis=0).astype(jnp.bfloat16)
    x = jnp.concatenate(
        [attn.reshape(PLANE, TOK, HD), jnp.broadcast_to(span_rows, (PLANE, 2 * SPZ, HD))], axis=1
    )
    x = exchange(x, plane_axes)
    y = merge(exchange(project(x, out_weight), "core"))
    y = exchange(y, "xh")
    span_mine = jnp.sum(y[:, TOK:].astype(jnp.float32).reshape(2 * NXH, SPZ, COLS), axis=0)
    spans = exchange(
        jnp.broadcast_to(span_mine, (NZ, SPZ, COLS)), "z"
    ).reshape(SEGS, COLS)
    return finalize(scalars, y, spans, seg_lengths, lang_ids)


def solution(mesh):
    split = Mesh(
        mesh.devices.reshape(NZ, NXL, NY, NXH, NCORE), ("z", "xl", "y", "xh", "core")
    )
    seq = ("z", "xl", "y")
    head = ("xh", "core")
    in_specs = (
        P(seq, head),
        P(seq, head),
        P(seq, head),
        P(head, None),
        P(),
        P(),
        P(),
    )
    out_specs = (P(seq, head), P(None, head))
    return jax.shard_map(
        on_device, mesh=split, in_specs=in_specs, out_specs=out_specs, check_vma=False
    )
```

time: 819 us -> 142 us (0.17)
  waiting for transfers between devices: 623 us -> 35.7 us
  starting transfers between devices: 140 us -> 23.1 us
  blocking collectives: 0 us -> 49.2 us
  matrix products: 23.7 us -> 0 us
  Pallas kernels: 0 us -> 20.8 us
  between operations: 15.3 us -> 0.8 us
    psum x2 -> x0, waiting for transfers between devices: 608 us -> none  [the longest x1 561 us: on_device(): span_sum = lax.psum(span_part, 'seq')]
    ppermute x32 -> x4, starting transfers between devices: 140 us -> 9.07 us  [shifted(): return lax.ppermute(block, axis, route)]
    all_to_all x0 -> x4, blocking collectives: none -> 49.2 us  [exchange(): return lax.all_to_all(x, axes, 0, 0, tiled=True)]
    dot_general x15 -> x0, matrix products: 23.7 us -> none  [the longest x5 7.5 us: absorb(): jnp.einsum('tkgd,nkd->kgtn', query_grid, key_block, preferred_element_typ...]
    pallas_call x0 -> x4, Pallas kernels: none -> 20.8 us  [the longest x1 9.48 us: attention(): pl.pallas_call(attn_kernel, out_shape=(jax.ShapeDtypeStruct((T, HD), jnp....]
    all_to_all x0 -> x3, starting transfers between devices: none -> 14.1 us  [exchange(): return lax.all_to_all(x, axes, 0, 0, tiled=True)]
    all_to_all x0 -> x3, waiting for transfers between devices: none -> 10.4 us  [exchange(): return lax.all_to_all(x, axes, 0, 0, tiled=True)]
    ppermute x32 -> x4, waiting for transfers between devices: 15 us -> 25.3 us  [shifted(): return lax.ppermute(block, axis, route)]
  transfers between devices with their start and end apart: 34 -> 7, of which waited for: 4 -> 5; matrix products, arithmetic and copies ran while one was open for 1% -> 3% of each run, Pallas kernels for 0% -> 0%
where the time goes in v1:
time: 142 us; the launch traced here: 140 us
  blocking collectives  49.2 us (35%)
  waiting for transfers between devices  35.7 us (25%)
  starting transfers between devices  23.1 us (16%)
  Pallas kernels  20.8 us (15%)
  local copies, waits for them, and re-layouts  7.35 us (5%)
  other arithmetic  3.47 us (2%)
    all_to_all x4, blocking collectives, exchange(): return lax.all_to_all(x, axes, 0, 0, tiled=True)  49.2 us
    ppermute x4, waiting for transfers between devices, shifted(): return lax.ppermute(block, axis, route)  25.3 us
    all_to_all x3, starting transfers between devices, exchange(): return lax.all_to_all(x, axes, 0, 0, tiled=True)  14.1 us
    all_to_all x3, waiting for transfers between devices, exchange(): return lax.all_to_all(x, axes, 0, 0, tiled=True)  10.4 us
    pallas_call x1, Pallas kernels, attention(): pl.pallas_call(attn_kernel, out_shape=(jax.ShapeDtypeStruct((T, HD), jnp....  9.48 us
    ppermute x4, starting transfers between devices, shifted(): return lax.ppermute(block, axis, route)  9.07 us
    pallas_call x1, Pallas kernels, project(): pl.pallas_call(proj_kernel, grid=(NXH * NCORE,), out_shape=jax.ShapeDtype...  6.52 us
  transfers between devices with their start and end apart: 7, of which 5 were waited for; matrix products, arithmetic and copies ran while one was open for 3% of the time, Pallas kernels for 0%

profile of v1, /device:TPU:4, one launch (start us, length us, event | category | flops | bytes accessed | tf_op | source)
XLA Modules:
  0.0 140.4 jit_solution(12080369267331093611)
XLA Ops:
  0.6 0.0 copy-start
  0.6 0.8 fusion.1
  1.5 0.8 fusion
  2.3 0.8 broadcast_in_dim.15
  3.1 5.1 %all-to-all-start = ((bf16[8,128,256]{2,1,0:T(8,128)(2,1)}), bf16[8,128,256]{2,1,0:T(8,128)(2,1)S(1)}, u32[]{:S(2)}, u32[]{:S(2)}) async-start(bf16[8,128,256]{2,1,0:T(8,128)(2,1)} %bitcast.4), calls=%async_computation | async-start | bytes 1048576 | tf_op jit(solution)/shard_map/all_to_all | solution.py:242
  8.2 5.2 %collective-permute-start.2 = (bf16[2,128,256]{2,1,0:T(8,128)(2,1)S(1)}, bf16[2,128,256]{2,1,0:T(8,128)(2,1)S(1)}, u32[]{:S(2)}, u32[]{:S(2)}) collective-permute-start(bf16[2,128,256]{2,1,0:T(8,128)(2,1)S(1)} %pad_maximum_fusion.2), channel_id=1, source_target_pairs={{0,64},{32,96},{64,128},{96,160},{128,192},{160,224},{1,65},{33,97... | collective-permute-start | bytes 393224 | tf_op jit(solution)/shard_map/ppermute | solution.py:238
  13.4 1.3 collective-permute-start.3
  14.7 0.0 copy-done
  14.8 1.1 collective-permute-done.2
  15.9 9.6 %collective-permute-done.3 = bf16[2,128,256]{2,1,0:T(8,128)(2,1)S(1)} collective-permute-done((bf16[2,128,256]{2,1,0:T(8,128)(2,1)S(1)}, bf16[2,128,256]{2,1,0:T(8,128)(2,1)S(1)}, u32[]{:S(2)}, u32[]{:S(2)}) %collective-permute-start.3) | collective-permute-done | bytes 131104 | tf_op jit(solution)/shard_map/ppermute | solution.py:238
  25.6 1.3 pad_maximum_fusion
  26.9 0.0 copy-start.9
  26.9 0.0 all-to-all-done
  26.9 5.6 %all-to-all-start.1 = ((bf16[8,128,640]{2,1,0:T(8,128)(2,1)}), bf16[8,128,640]{2,1,0:T(8,128)(2,1)S(1)}, u32[]{:S(2)}, u32[]{:S(2)}) async-start(bf16[8,128,640]{2,1,0:T(8,128)(2,1)} %pad_maximum_fusion), calls=%async_computation.1 | async-start | bytes 2621440 | tf_op jit(solution)/shard_map/all_to_all | solution.py:242
  32.4 1.3 collective-permute-start
  33.7 0.0 copy-done.3
  33.7 1.3 collective-permute-start.1
  35.1 0.0 copy-done.9
  35.1 0.6 dynamic_slice.4
  35.7 1.2 pad_add_fusion.sc_ref
  36.9 7.7 %collective-permute-done.dn_ref = bf16[1024,256]{1,0:T(8,128)(2,1)S(1)} collective-permute-done((bf16[1024,256]{1,0:T(8,128)(2,1)S(1)}, bf16[1024,256]{1,0:T(8,128)(2,1)S(1)}, u32[]{:S(2)}, u32[]{:S(2)}) %collective-permute-start) | collective-permute-done | bytes 524320 | tf_op jit(solution)/shard_map/ppermute | solution.py:238
  44.6 0.0 copy-start.5
  44.6 6.8 %collective-permute-done.1.up_ref = bf16[1024,256]{1,0:T(8,128)(2,1)S(1)} collective-permute-done((bf16[1024,256]{1,0:T(8,128)(2,1)S(1)}, bf16[1024,256]{1,0:T(8,128)(2,1)S(1)}, u32[]{:S(2)}, u32[]{:S(2)}) %collective-permute-start.1) | collective-permute-done | bytes 524320 | tf_op jit(solution)/shard_map/ppermute | solution.py:238
  51.4 0.0 copy-start.6
  51.4 0.0 all-to-all-done.1
  51.4 0.0 copy-start.1
  51.4 0.0 copy-done.5
  51.4 0.8 copy-done.6
  52.2 0.4 copy-done.1
  52.7 9.5 %window_attention.1 = (bf16[1024,128]{1,0:T(8,128)(2,1)}, f32[64,128]{1,0:T(8,128)}) custom-call(s32[3]{0:T(128)} %pad_add_fusion.sc_ref, bf16[1024,256]{1,0:T(8,128)(2,1)} %bitcast.32, bf16[1024,256]{1,0:T(8,128)(2,1)} %copy-done.5, bf16[1024,256]{1,0:T(8,128)(2,1)} %copy-done.6, bf16[1024,640]{1,0:T(8,128)(2,1)} %bitcast.27, s32[1,64]{1,0:T(1,128)} %bitcast.37), custom_call_target="tpu_custom_call" | custom-call | tf_op jit(solution)/shard_map/window_attention/pallas_call | solution.py:121
  62.1 15.6 %all_to_all.35 = f32[8,8,128]{2,1,0:T(8,128)S(1)} all-to-all(f32[8,8,128]{2,1,0:T(8,128)} %bitcast.36), channel_id=1, replica_groups=mesh['z'=8,'xl'=2,'y'=4,'xh'=2,'core'=2] {'z'}, dimensions={0} | all-to-all | bytes 65536 | tf_op jit(solution)/shard_map/all_to_all | solution.py:242
  77.8 1.0 pad_maximum_fusion.1
  78.8 14.1 %all_to_all.36.x_ref = bf16[8,144,128]{2,1,0:T(8,128)(2,1)} all-to-all(bf16[8,144,128]{2,1,0:T(8,128)(2,1)S(1)} %pad_maximum_fusion.1), channel_id=1, replica_groups=mesh['z'=8,'xl'=2,'y'=4,'xh'=2,'core'=2] {'xl','y'}, dimensions={0} | all-to-all | bytes 589824 | tf_op jit(solution)/shard_map/all_to_all | solution.py:242
  92.8 6.5 %projection.1 = bf16[2,2,144,1024]{3,2,1,0:T(8,128)(2,1)} custom-call(bf16[8,144,128]{2,1,0:T(8,128)(2,1)} %all_to_all.36.x_ref, bf16[1024,4096]{1,0:T(8,128)(2,1)} %w_ref.1), custom_call_target="tpu_custom_call" | custom-call | tf_op jit(solution)/shard_map/projection/pallas_call | solution.py:155
  99.3 6.7 %all_to_all.37.y_ref = bf16[2,2,144,1024]{3,2,1,0:T(8,128)(2,1)} all-to-all(bf16[2,2,144,1024]{3,2,1,0:T(8,128)(2,1)} %projection.1), channel_id=1, replica_groups=mesh['z'=8,'xl'=2,'y'=4,'xh'=2,'core'=2] {'core'}, dimensions={0} | all-to-all | bytes 2359296 | tf_op jit(solution)/shard_map/all_to_all | solution.py:242
  106.1 2.0 %merge.1 = bf16[2,144,1024]{2,1,0:T(8,128)(2,1)} custom-call(bf16[2,2,144,1024]{3,2,1,0:T(8,128)(2,1)} %all_to_all.37.y_ref), custom_call_target="tpu_custom_call" | custom-call | tf_op jit(solution)/shard_map/merge/pallas_call | solution.py:176
  108.1 0.0 copy-start.7
  108.1 12.8 %all_to_all.38.y_ref = bf16[2,144,1024]{2,1,0:T(8,128)(2,1)S(1)} all-to-all(bf16[2,144,1024]{2,1,0:T(8,128)(2,1)} %merge.1), channel_id=1, replica_groups=mesh['z'=8,'xl'=2,'y'=4,'xh'=2,'core'=2] {'xh'}, dimensions={0} | all-to-all | bytes 1179648 | tf_op jit(solution)/shard_map/all_to_all | solution.py:242
  121.0 0.8 broadcast_in_dim.19
  121.8 3.4 %all-to-all-start.6 = ((f32[8,8,1024]{2,1,0:T(8,128)}), f32[8,8,1024]{2,1,0:T(8,128)S(1)}, u32[]{:S(2)}, u32[]{:S(2)}) async-start(f32[8,8,1024]{2,1,0:T(8,128)} %broadcast_in_dim.19), calls=%async_computation.6 | async-start | bytes 524288 | tf_op jit(solution)/shard_map/all_to_all | solution.py:242
  125.2 0.0 copy-done.7
  125.2 0.7 copy.10.lenc_ref
  125.9 0.0 copy-done.8
  125.9 0.7 copy.11.idc_ref
  126.6 10.4 %all-to-all-done.6 = f32[8,8,1024]{2,1,0:T(8,128)S(1)} async-done(((f32[8,8,1024]{2,1,0:T(8,128)}), f32[8,8,1024]{2,1,0:T(8,128)S(1)}, u32[]{:S(2)}, u32[]{:S(2)}) %all-to-all-start.6) | async-done | bytes 262176 | tf_op jit(solution)/shard_map/all_to_all | solution.py:242
  137.0 0.0 copy-done.2
  137.0 0.7 copy-done.4
  137.7 2.8 %centre.1 = (bf16[128,1024]{1,0:T(8,128)(2,1)}, f32[64,1024]{1,0:T(8,128)}) custom-call(s32[3]{0:T(128)} %pad_add_fusion.sc_ref, bf16[2,144,1024]{2,1,0:T(8,128)(2,1)} %copy-done.2, f32[64,1024]{1,0:T(8,128)} %bitcast.33, s32[1,64]{1,0:T(1,128)} %bitcast.38, s32[64,1]{1,0:T(8,128)} %copy.10.lenc_ref, s32[1,64]{1,0:T(1,128)} %bitcast.40, s32[64,1]{1,0:T(8,128)} %copy.11.idc_ref), custom_call_target="tpu_custom_call" | custom-call | tf_op jit(solution)/shard_map/centre/pallas_call | solution.py:215
  (15 shorter events, 0.2 us)
Async XLA Ops:
  0.6 14.1 %copy-start = (bf16[128,1024]{1,0:T(8,128)(2,1)S(1)}, bf16[128,1024]{1,0:T(8,128)(2,1)}, u32[]{:S(2)}) copy-start(bf16[128,1024]{1,0:T(8,128)(2,1)} %param.7) | copy-start | bytes 786436
  3.1 23.7 %all-to-all-start = ((bf16[8,128,256]{2,1,0:T(8,128)(2,1)}), bf16[8,128,256]{2,1,0:T(8,128)(2,1)S(1)}, u32[]{:S(2)}, u32[]{:S(2)}) async-start(bf16[8,128,256]{2,1,0:T(8,128)(2,1)} %bitcast.4), calls=%async_computation | async-start | bytes 1048576 | tf_op jit(solution)/shard_map/all_to_all | solution.py:242
  8.2 7.7 %collective-permute-start.2 = (bf16[2,128,256]{2,1,0:T(8,128)(2,1)S(1)}, bf16[2,128,256]{2,1,0:T(8,128)(2,1)S(1)}, u32[]{:S(2)}, u32[]{:S(2)}) collective-permute-start(bf16[2,128,256]{2,1,0:T(8,128)(2,1)S(1)} %pad_maximum_fusion.2), channel_id=1, source_target_pairs={{0,64},{32,96},{64,128},{96,160},{128,192},{160,224},{1,65},{33,97... | collective-permute-start | bytes 393224 | tf_op jit(solution)/shard_map/ppermute | solution.py:238
  13.4 12.1 %collective-permute-start.3 = (bf16[2,128,256]{2,1,0:T(8,128)(2,1)S(1)}, bf16[2,128,256]{2,1,0:T(8,128)(2,1)S(1)}, u32[]{:S(2)}, u32[]{:S(2)}) collective-permute-start(bf16[2,128,256]{2,1,0:T(8,128)(2,1)S(1)} %pad_maximum_fusion.2), channel_id=1, source_target_pairs={{64,0},{96,32},{128,64},{160,96},{192,128},{224,160},{65,1},{97,33... | collective-permute-start | bytes 393224 | tf_op jit(solution)/shard_map/ppermute | solution.py:238
  26.9 8.2 %copy-start.9 = (s32[32]{0:T(128)S(1)}, s32[32]{0:T(128)}, u32[]{:S(2)}) copy-start(s32[32]{0:T(128)} %param.11) | copy-start | bytes 388
  26.9 6.9 %copy-start.3 = (bf16[8,128,256]{2,1,0:T(8,128)(2,1)}, bf16[8,128,256]{2,1,0:T(8,128)(2,1)S(1)}, u32[]{:S(2)}) copy-start(bf16[8,128,256]{2,1,0:T(8,128)(2,1)S(1)} %all-to-all-done) | copy-start | bytes 1572868
  26.9 24.6 %all-to-all-start.1 = ((bf16[8,128,640]{2,1,0:T(8,128)(2,1)}), bf16[8,128,640]{2,1,0:T(8,128)(2,1)S(1)}, u32[]{:S(2)}, u32[]{:S(2)}) async-start(bf16[8,128,640]{2,1,0:T(8,128)(2,1)} %pad_maximum_fusion), calls=%async_computation.1 | async-start | bytes 2621440 | tf_op jit(solution)/shard_map/all_to_all | solution.py:242
  32.4 12.2 %collective-permute-start = (bf16[1024,256]{1,0:T(8,128)(2,1)S(1)}, bf16[1024,256]{1,0:T(8,128)(2,1)S(1)}, u32[]{:S(2)}, u32[]{:S(2)}) collective-permute-start(bf16[1024,256]{1,0:T(8,128)(2,1)S(1)} %bitcast.30), channel_id=1, source_target_pairs={{0,32},{32,64},{64,96},{96,128},{128,160},{160,192},{192,224},{1,3... | collective-permute-start | bytes 1572872 | tf_op jit(solution)/shard_map/ppermute | solution.py:238
  33.7 17.7 %collective-permute-start.1 = (bf16[1024,256]{1,0:T(8,128)(2,1)S(1)}, bf16[1024,256]{1,0:T(8,128)(2,1)S(1)}, u32[]{:S(2)}, u32[]{:S(2)}) collective-permute-start(bf16[1024,256]{1,0:T(8,128)(2,1)S(1)} %bitcast.31), channel_id=1, source_target_pairs={{32,0},{64,32},{96,64},{128,96},{160,128},{192,160},{224,192},{33,... | collective-permute-start | bytes 1572872 | tf_op jit(solution)/shard_map/ppermute | solution.py:238
  44.6 6.8 %copy-start.5 = (bf16[1024,256]{1,0:T(8,128)(2,1)}, bf16[1024,256]{1,0:T(8,128)(2,1)S(1)}, u32[]{:S(2)}) copy-start(bf16[1024,256]{1,0:T(8,128)(2,1)S(1)} %collective-permute-done.dn_ref) | copy-start | bytes 1572868
  51.4 0.8 copy-start.6
  51.4 1.2 copy-start.1
  108.1 17.1 %copy-start.7 = (s32[64]{0:T(128)S(1)}, s32[64]{0:T(128)}, u32[]{:S(2)}) copy-start(s32[64]{0:T(128)} %param.12) | copy-start | bytes 772
  108.1 17.8 %copy-start.8 = (s32[64]{0:T(128)S(1)}, s32[64]{0:T(128)}, u32[]{:S(2)}) copy-start(s32[64]{0:T(128)} %param.13) | copy-start | bytes 772
  120.9 16.1 %copy-start.2 = (bf16[2,144,1024]{2,1,0:T(8,128)(2,1)}, bf16[2,144,1024]{2,1,0:T(8,128)(2,1)S(1)}, u32[]{:S(2)}) copy-start(bf16[2,144,1024]{2,1,0:T(8,128)(2,1)S(1)} %all_to_all.38.y_ref) | copy-start | bytes 1769476
  121.8 15.2 %all-to-all-start.6 = ((f32[8,8,1024]{2,1,0:T(8,128)}), f32[8,8,1024]{2,1,0:T(8,128)S(1)}, u32[]{:S(2)}, u32[]{:S(2)}) async-start(f32[8,8,1024]{2,1,0:T(8,128)} %broadcast_in_dim.19), calls=%async_computation.6 | async-start | bytes 524288 | tf_op jit(solution)/shard_map/all_to_all | solution.py:242
  137.0 0.7 copy-start.4
